TPU v7x, 32 devices: a whole 2x2x4 slice. The times are simulated.
32 devices in a mesh: orb: 16 (over z, x, core), aux: 2 (over y).
Axes of the slice: x: 2, y: 2, z: 4, core: 2. Of those that a mesh axis runs over, the one named last changes fastest.
Arguments:
- three_index: float32 [56, 1024, 2048], P(None, 'aux', 'orb'), may hold values from -0.5 to 0.5
- pair_density: float32 [3136, 3136], P('orb'), as said below
- active_orbitals: int32 [56], replicated, may hold values from 200 to 2047, as said below
- screen_mask: int32 [64, 128], P('aux', 'orb'), may hold values from 0 to 1
- one_density: float32 [56, 56], replicated
- inactive_fock: float32 [2048, 256], P('orb'), may hold values from -6 to 6
- active_fock: float32 [2048, 200], P('orb'), may hold values from -6 to 6
Outputs:
- rotation_gradient: float32 [2048, 256], P(('orb', 'aux'))
Inputs may be any that keep to these rules, and one draw needn't show every extreme that they name: `active_orbitals`: 56 distinct orbital indices. pair_density is symmetric: its entry at (tu, vw) equals that at (vw, tu).
All inputs are finite; a program needn't handle non-finite values.
Results may differ from a plain program's by a relative error of at most 0.0001.
Values sent between devices are 32-bit elements; how exact they have to be, the bound alone decides.
No kernel may reach another device: no remote copies, remote signals or barrier semaphores. Data moves between devices by JAX's collectives and lax.ppermute only.
A program may use at most 128 MiB of HBM per device.

v0:
```python
import jax
import jax.numpy as jnp
from jax import lax
from jax.sharding import PartitionSpec as P


def shards(
    three_index, pair_density, active_orbitals, screen_mask, one_density, inactive_fock, active_fock
):
    highest = lax.Precision.HIGHEST
    act_count = three_index.shape[0]
    slab_count = three_index.shape[1]
    row_count = three_index.shape[2]
    inactive_count = active_fock.shape[1]
    orb_position = lax.axis_index("orb")
    kept_mask = jnp.repeat(
        jnp.repeat(screen_mask.astype(jnp.float32), slab_count // screen_mask.shape[0], axis=0),
        row_count // screen_mask.shape[1],
        axis=1,
    )
    screened = three_index * kept_mask[None]
    global_rows = orb_position * row_count + jnp.arange(row_count, dtype=jnp.int32)
    active_pick = (global_rows[:, None] == active_orbitals[None, :]).astype(jnp.float32)
    partial_pairs = jnp.einsum("wPp,pv->Pvw", screened, active_pick, precision=highest).reshape(
        slab_count, act_count * act_count
    )
    pairs = lax.psum(partial_pairs, "orb")
    column_block = jnp.dot(pairs, pair_density.T, precision=highest)
    half = lax.all_gather(column_block, "orb", axis=1, tiled=True)
    q_partial = jnp.einsum(
        "uPp,Ptu->pt", screened, half.reshape(slab_count, act_count, act_count), precision=highest
    )
    occ_index = jnp.concatenate([jnp.arange(inactive_count, dtype=jnp.int32), active_orbitals])
    row_share = row_count // lax.axis_size("aux")
    aux_offset = lax.axis_index("aux") * row_share
    qmatrix = lax.psum(q_partial, "aux")
    inactive_cols = 2.0 * (inactive_fock[:, :inactive_count] + active_fock)
    active_cols = (
        jnp.dot(inactive_fock[:, inactive_count:], one_density, precision=highest) + qmatrix
    )
    fock = jnp.concatenate([inactive_cols, active_cols], axis=1)
    occ_pick = (global_rows[:, None] == occ_index[None, :]).astype(jnp.float32)
    occupied = lax.psum(jnp.dot(occ_pick.T, fock, precision=highest), "orb")
    fock_mine = lax.dynamic_slice_in_dim(fock, aux_offset, row_share, 0)
    pick_mine = lax.dynamic_slice_in_dim(occ_pick, aux_offset, row_share, 0)
    transposed = jnp.dot(pick_mine, occupied.T, precision=highest)
    return 2.0 * (fock_mine - transposed)


def solution(mesh):
    in_specs = (
        P(None, "aux", "orb"),
        P("orb", None),
        P(),
        P("aux", "orb"),
        P(),
        P("orb", None),
        P("orb", None),
    )
    out_specs = P(("orb", "aux"), None)
    return jax.shard_map(shards, mesh=mesh, in_specs=in_specs, out_specs=out_specs, check_vma=False)
```

profile of v0, /device:TPU:1, one launch (start us, length us, event | category | flops | bytes accessed | tf_op | source)
XLA Modules:
  0.0 370.7 jit_solution(4190907556177980599)
XLA Ops:
  6.5 0.0 copy-start
  6.5 0.0 all-reduce.3.cloned.1.call-start
  6.5 0.8 convert_element_type.2
  7.4 0.1 broadcast_in_dim.4
  7.5 0.1 reshape.16
  7.6 0.1 copy.22
  7.8 13.5 %fusion.7 = f32[512,56,56]{0,1,2:T(8,128)S(1)} fusion(f32[56,512,128]{2,1,0:T(8,128)} %param.7, f32[512,128]{1,0:T(8,128)S(1)} %copy.22, s32[128]{0:T(128)S(1)} %iota_add_fusion, s32[56]{0:T(128)} %param.9), kind=kOutput, calls=%fused_computation.7 | convolution fusion | flops 2469927936 | bytes 21365472 | tf_op jit(solution)/shard_map/wPp,pv->Pvw/dot_general | solution.py:24
  21.2 6.4 %copy.23 = f32[512,56,56]{0,2,1:T(8,128)} copy(f32[512,56,56]{0,1,2:T(8,128)S(1)} %fusion.7) | data formatting | bytes 12845056 | tf_op jit(solution)/shard_map/wPp,pv->Pvw/transpose | solution.py:24
  27.6 0.0 all-reduce.3.cloned.1.call-update
  27.6 0.0 copy-start.2
  27.6 0.0 copy-start.4
  27.6 0.0 copy-start.1
  27.7 0.2 all-gather.3.cloned.1.call-start
  27.9 143.9 %all-reduce.3.cloned.1.call-done = f32[512,3136]{0,1:T(8,128)} async-done(((f32[512,3136]{0,1:T(8,128)}), f32[512,3136]{0,1:T(8,128)}) %all-reduce.3.cloned.1.call-update) | async-done | bytes 6422544 | tf_op jit(solution)/shard_map/psum | solution.py:27
  171.8 0.0 copy-done
  171.8 8.6 %convolution_bitcast_fusion = f32[1,196,512]{2,1,0:T(8,128)} fusion(f32[512,3136]{0,1:T(8,128)} %all-reduce.3.cloned.1.call-done, f32[196,3136]{1,0:T(8,128)S(1)} %copy-done), kind=kOutput, calls=%fused_computation.8 | convolution fusion | flops 3776446464 | bytes 9282560 | tf_op jit(solution)/shard_map/dot_general | solution.py:28
  180.4 0.0 all-gather.3.cloned.1.call-update
  180.4 0.0 all-reduce.5.cloned.1.call-start
  180.5 0.0 copy-done.2
  180.5 0.1 copy.21
  180.6 0.0 copy-done.4
  180.6 0.1 pad_add_fusion
  180.7 0.0 copy-done.1
  180.7 63.3 %all-gather.3.cloned.1.call-done = f32[16,196,512]{2,1,0:T(8,128)} async-done(((f32[1,196,512]{2,1,0:T(8,128)}), f32[16,196,512]{2,1,0:T(8,128)}) %all-gather.3.cloned.1.call-update) | async-done | bytes 6422544 | tf_op jit(solution)/shard_map/all_gather | solution.py:29
  244.0 6.1 %reshape.20 = f32[3136,512]{1,0:T(8,128)} reshape(f32[16,196,512]{2,1,0:T(8,128)} %all-gather.3.cloned.1.call-done) | data formatting | bytes 12845056
  250.2 0.0 copy-start.3
  250.2 15.4 %fusion.11 = f32[128,56]{0,1:T(8,128)S(1)} fusion(f32[512,56,56]{0,2,1:T(8,128)} %bitcast.23, f32[56,512,128]{2,1,0:T(8,128)} %param.7, f32[512,128]{1,0:T(8,128)S(1)} %copy.22), kind=kOutput, calls=%fused_computation.11 | convolution fusion | flops 2469920768 | bytes 21393408 | tf_op jit(solution)/shard_map/uPp,Ptu->pt/dot_general | solution.py:30
  265.5 6.3 %psum.22 = f32[128,56]{0,1:T(8,128)S(1)} all-reduce(f32[128,56]{0,1:T(8,128)S(1)} %fusion.11), channel_id=1, replica_groups=mesh['orb'=16,'aux'=2] {'aux'}, use_global_device_ids=true, to_apply=%region_1.0 | all-reduce | flops 7168 | bytes 57344 | tf_op jit(solution)/shard_map/psum | solution.py:36
  271.8 0.0 copy-done.3
  271.8 0.3 convolution_add_fusion
  272.2 0.1 copy.25
  272.3 1.1 fusion.16
  273.4 0.0 all-reduce.5.cloned.1.call-update
  273.4 0.1 broadcast_compare_fusion
  273.5 88.9 %all-reduce.5.cloned.1.call-done = f32[256,256]{1,0:T(8,128)} async-done(((f32[256,256]{1,0:T(8,128)}), f32[256,256]{1,0:T(8,128)}) %all-reduce.5.cloned.1.call-update) | async-done | bytes 262160 | tf_op jit(solution)/shard_map/psum | solution.py:43
  362.3 1.9 fusion.10
  (4 shorter events, 0.0 us)
Async XLA Ops:
  6.5 165.2 %copy-start = (f32[196,3136]{1,0:T(8,128)S(1)}, f32[196,3136]{1,0:T(8,128)}, u32[]{:S(2)}) copy-start(f32[196,3136]{1,0:T(8,128)} %param.8) | copy-start | bytes 7375876
  6.5 165.2 %all-reduce.3.cloned.1.call-start = ((), (), s32[]{:S(2)}) async-start(), calls=%async_computation | async-start | bytes 12845056 | tf_op jit(solution)/shard_map/psum | solution.py:27
  27.6 152.8 %copy-start.2 = (f32[128,200]{0,1:T(8,128)S(1)}, f32[128,200]{0,1:T(8,128)}, u32[]{:S(2)}) copy-start(f32[128,200]{0,1:T(8,128)} %param.13) | copy-start | bytes 307204
  27.6 153.0 %copy-start.4 = (s32[56]{0:T(128)S(1)}, s32[56]{0:T(128)}, u32[]{:S(2)}) copy-start(s32[56]{0:T(128)} %param.9) | copy-start | bytes 676
  27.6 153.0 %copy-start.1 = (f32[128,256]{1,0:T(8,128)S(1)}, f32[128,256]{1,0:T(8,128)}, u32[]{:S(2)}) copy-start(f32[128,256]{1,0:T(8,128)} %param.12) | copy-start | bytes 393220
  27.7 216.4 %all-gather.3.cloned.1.call-start = ((), (), s32[]{:S(2)}) async-start(), calls=%async_computation.2 | async-start | bytes 6963200 | tf_op jit(solution)/shard_map/all_gather | solution.py:29
  180.4 181.9 %all-reduce.5.cloned.1.call-start = ((), (), s32[]{:S(2)}) async-start(), calls=%async_computation.1 | async-start | bytes 524288 | tf_op jit(solution)/shard_map/psum | solution.py:43
  250.2 21.7 %copy-start.3 = (f32[56,56]{1,0:T(8,128)S(1)}, f32[56,56]{1,0:T(8,128)}, u32[]{:S(2)}) copy-start(f32[56,56]{1,0:T(8,128)} %param.11) | copy-start | bytes 37636
Sparse Core Ops, SparseCore 0:
  27.7 143.9 all-reduce.2
  180.5 63.4 all-gather.2
  273.5 88.8 all-reduce.4
where the time goes:
time: 371 us
  waiting for transfers between devices  296 us (80%)
  matrix products  40.7 us (11%)
  between operations  13.2 us (4%)
  local copies, waits for them, and re-layouts  13 us (4%)
  blocking collectives  6.31 us (2%)
    psum x1, waiting for transfers between devices, shards(): pairs = lax.psum(partial_pairs, 'orb')  144 us
    psum x1, waiting for transfers between devices, shards(): occupied = lax.psum(jnp.dot(occ_pick.T, fock, precision=highest), 'orb')  88.9 us
    all_gather x1, waiting for transfers between devices, shards(): half = lax.all_gather(column_block, 'orb', axis=1, tiled=True)  63.3 us
    dot_general x1, matrix products, shards(): jnp.einsum('uPp,Ptu->pt', screened, half.reshape(slab_count, act_count, a...  15.4 us
    dot_general x1, matrix products, shards(): jnp.einsum('wPp,pv->Pvw', screened, active_pick, precision=highest)  13.5 us
    dot_general x1, matrix products, shards(): column_block = jnp.dot(pairs, pair_density.T, precision=highest)  8.61 us
  transfers between devices with their start and end apart: 3, of which 3 were waited for; matrix products, arithmetic and copies ran while one was open for 0% of the time, Pallas kernels for 0%

commit v1 on v0

--- a/solution.py
+++ b/solution.py
@@ -24,7 +24,9 @@
     partial_pairs = jnp.einsum("wPp,pv->Pvw", screened, active_pick, precision=highest).reshape(
         slab_count, act_count * act_count
     )
-    pairs = lax.psum(partial_pairs, "orb")
+    pairs = partial_pairs
+    for hop in (1, 2, 4, 8):
+        pairs = pairs + lax.ppermute(pairs, "orb", [(dev, dev ^ hop) for dev in range(16)])
     column_block = jnp.dot(pairs, pair_density.T, precision=highest)
     half = lax.all_gather(column_block, "orb", axis=1, tiled=True)
     q_partial = jnp.einsum(

time: 371 us -> 804 us (2.17)
  waiting for transfers between devices: 296 us -> 717 us
  other arithmetic: 1.02 us -> 12 us
    ppermute x0 -> x4, waiting for transfers between devices: none -> 563 us  [shards(): lax.ppermute(pairs, 'orb', [(dev, dev ^ hop) for dev in range(16)])]
    psum x1 -> x0, waiting for transfers between devices: 144 us -> none  [shards(): pairs = lax.psum(partial_pairs, 'orb')]
    add x0 -> x3, other arithmetic: none -> 11 us  [shards(): pairs + lax.ppermute(pairs, 'orb', [(dev, dev ^ hop) for dev in range(16)])]
  transfers between devices with their start and end apart: 3 -> 6, of which waited for: 3 -> 6; matrix products, arithmetic and copies ran while one was open for 0% -> 0% of each run, Pallas kernels for 0% -> 0%
where the time goes in v1:
time: 804 us
  waiting for transfers between devices  717 us (89%)
  matrix products  38.7 us (5%)
  between operations  13.6 us (2%)
  other arithmetic  12 us (1%)
  local copies, waits for them, and re-layouts  10.4 us (1%)
    ppermute x4, waiting for transfers between devices, shards(): lax.ppermute(pairs, 'orb', [(dev, dev ^ hop) for dev in range(16)])  563 us
    psum x1, waiting for transfers between devices, shards(): occupied = lax.psum(jnp.dot(occ_pick.T, fock, precision=highest), 'orb')  88.8 us
    all_gather x1, waiting for transfers between devices, shards(): half = lax.all_gather(column_block, 'orb', axis=1, tiled=True)  64.9 us
  transfers between devices with their start and end apart: 6, of which 6 were waited for; matrix products, arithmetic and copies ran while one was open for 0% of the time, Pallas kernels for 0%

profile of v1, /device:TPU:1, one launch (start us, length us, event | category | flops | bytes accessed | tf_op | source)
XLA Modules:
  0.0 803.5 jit_solution(17214977238317419113)
XLA Ops:
  6.5 0.0 copy-start
  6.5 0.0 all-gather.3.cloned.1.call-start
  6.5 0.8 convert_element_type.2
  7.4 0.1 broadcast_in_dim.4
  7.5 0.1 reshape.16
  7.6 0.1 copy.22
  7.8 13.6 %fusion.9 = f32[512,56,56]{0,1,2:T(8,128)S(1)} fusion(f32[56,512,128]{2,1,0:T(8,128)} %param.7, f32[512,128]{1,0:T(8,128)S(1)} %copy.22, s32[128]{0:T(128)S(1)} %iota_add_fusion, s32[56]{0:T(128)} %param.9), kind=kOutput, calls=%fused_computation.9 | convolution fusion | flops 2469927936 | bytes 21365472 | tf_op jit(solution)/shard_map/wPp,pv->Pvw/dot_general | solution.py:24
  21.4 3.7 copy.23
  25.1 0.1 collective-permute-start
  25.2 10.4 %collective-permute-done = f32[512,3136]{0,1:T(8,128)} collective-permute-done((f32[512,3136]{0,1:T(8,128)S(1)}, f32[512,3136]{0,1:T(8,128)}, u32[]{:S(2)}, u32[]{:S(2)}) %collective-permute-start) | collective-permute-done | bytes 6422560 | tf_op jit(solution)/shard_map/ppermute | solution.py:29
  35.6 3.6 bitcast_add_fusion
  39.3 2.4 collective-permute-start.1
  41.7 138.5 %collective-permute-done.1 = f32[512,3136]{0,1:T(8,128)} collective-permute-done((f32[512,3136]{0,1:T(8,128)S(1)}, f32[512,3136]{0,1:T(8,128)}, u32[]{:S(2)}, u32[]{:S(2)}) %collective-permute-start.1) | collective-permute-done | bytes 6422560 | tf_op jit(solution)/shard_map/ppermute | solution.py:29
  180.2 3.7 add.40
  183.8 1.3 collective-permute-start.2
  185.1 137.8 %collective-permute-done.2 = f32[512,3136]{0,1:T(8,128)} collective-permute-done((f32[512,3136]{0,1:T(8,128)S(1)}, f32[512,3136]{0,1:T(8,128)}, u32[]{:S(2)}, u32[]{:S(2)}) %collective-permute-start.2) | collective-permute-done | bytes 6422560 | tf_op jit(solution)/shard_map/ppermute | solution.py:29
  323.0 3.7 add.41
  326.6 0.0 copy-start.2
  326.7 0.0 copy-start.4
  326.7 0.0 copy-start.1
  326.7 2.0 collective-permute-start.3
  328.7 276.2 %collective-permute-done.3 = f32[512,3136]{0,1:T(8,128)S(1)} collective-permute-done((f32[512,3136]{0,1:T(8,128)S(1)}, f32[512,3136]{0,1:T(8,128)S(1)}, u32[]{:S(2)}, u32[]{:S(2)}) %collective-permute-start.3) | collective-permute-done | bytes 6422560 | tf_op jit(solution)/shard_map/ppermute | solution.py:29
  604.8 0.0 copy-done
  604.9 6.5 fusion.12
  611.3 0.0 all-gather.3.cloned.1.call-update
  611.3 0.0 all-reduce.2.cloned.1.call-start
  611.4 0.0 copy-done.2
  611.4 0.1 copy.21
  611.5 0.0 copy-done.4
  611.5 0.1 pad_add_fusion
  611.6 0.0 copy-done.1
  611.6 64.9 %all-gather.3.cloned.1.call-done = f32[16,196,512]{2,1,0:T(8,128)} async-done(((f32[1,196,512]{2,1,0:T(8,128)}), f32[16,196,512]{2,1,0:T(8,128)}) %all-gather.3.cloned.1.call-update) | async-done | bytes 6422544 | tf_op jit(solution)/shard_map/all_gather | solution.py:31
  676.5 6.1 reshape.20
  682.7 0.0 copy-start.3
  682.7 15.4 %fusion.16 = f32[128,56]{0,1:T(8,128)S(1)} fusion(f32[512,56,56]{0,2,1:T(8,128)} %bitcast.23, f32[56,512,128]{2,1,0:T(8,128)} %param.7, f32[512,128]{1,0:T(8,128)S(1)} %copy.22), kind=kOutput, calls=%fused_computation.13 | convolution fusion | flops 2469920768 | bytes 21393408 | tf_op jit(solution)/shard_map/uPp,Ptu->pt/dot_general | solution.py:32
  698.0 6.3 psum.14
  704.3 0.0 copy-done.3
  704.4 0.3 convolution_add_fusion
  704.7 0.1 copy.25
  704.8 1.1 fusion.21
  705.9 0.0 all-reduce.2.cloned.1.call-update
  705.9 0.1 broadcast_compare_fusion
  706.0 88.8 %all-reduce.2.cloned.1.call-done = f32[256,256]{1,0:T(8,128)} async-done(((f32[256,256]{1,0:T(8,128)}), f32[256,256]{1,0:T(8,128)}) %all-reduce.2.cloned.1.call-update) | async-done | bytes 262160 | tf_op jit(solution)/shard_map/psum | solution.py:45
  794.8 1.9 fusion.15
  (4 shorter events, 0.0 us)
Async XLA Ops:
  6.5 598.3 %copy-start = (f32[196,3136]{1,0:T(8,128)S(1)}, f32[196,3136]{1,0:T(8,128)}, u32[]{:S(2)}) copy-start(f32[196,3136]{1,0:T(8,128)} %param.8) | copy-start | bytes 7375876
  6.5 670.0 %all-gather.3.cloned.1.call-start = ((), (), s32[]{:S(2)}) async-start(), calls=%async_computation.1 | async-start | bytes 6963200 | tf_op jit(solution)/shard_map/all_gather | solution.py:31
  25.1 10.5 %collective-permute-start = (f32[512,3136]{0,1:T(8,128)S(1)}, f32[512,3136]{0,1:T(8,128)}, u32[]{:S(2)}, u32[]{:S(2)}) collective-permute-start(f32[512,3136]{0,1:T(8,128)S(1)} %bitcast.22), channel_id=1, source_target_pairs={{0,2},{2,0},{4,6},{6,4},{8,10},{10,8},{12,14},{14,12},{16,18},{18,... | collective-permute-start | bytes 19267592 | tf_op jit(solution)/shard_map/ppermute | solution.py:29
  39.3 140.9 %collective-permute-start.1 = (f32[512,3136]{0,1:T(8,128)S(1)}, f32[512,3136]{0,1:T(8,128)}, u32[]{:S(2)}, u32[]{:S(2)}) collective-permute-start(f32[512,3136]{0,1:T(8,128)S(1)} %bitcast_add_fusion), channel_id=1, source_target_pairs={{0,4},{2,6},{4,0},{6,2},{8,12},{10,14},{12,8},{14,10},{16,20},{18,... | collective-permute-start | bytes 19267592 | tf_op jit(solution)/shard_map/ppermute | solution.py:29
  183.8 139.1 %collective-permute-start.2 = (f32[512,3136]{0,1:T(8,128)S(1)}, f32[512,3136]{0,1:T(8,128)}, u32[]{:S(2)}, u32[]{:S(2)}) collective-permute-start(f32[512,3136]{0,1:T(8,128)S(1)} %add.40), channel_id=1, source_target_pairs={{0,8},{2,10},{4,12},{6,14},{8,0},{10,2},{12,4},{14,6},{16,24},{18,... | collective-permute-start | bytes 19267592 | tf_op jit(solution)/shard_map/ppermute | solution.py:29
  326.6 284.7 %copy-start.2 = (f32[128,200]{0,1:T(8,128)S(1)}, f32[128,200]{0,1:T(8,128)}, u32[]{:S(2)}) copy-start(f32[128,200]{0,1:T(8,128)} %param.13) | copy-start | bytes 307204
  326.7 284.9 %copy-start.4 = (s32[56]{0:T(128)S(1)}, s32[56]{0:T(128)}, u32[]{:S(2)}) copy-start(s32[56]{0:T(128)} %param.9) | copy-start | bytes 676
  326.7 284.9 %copy-start.1 = (f32[128,256]{1,0:T(8,128)S(1)}, f32[128,256]{1,0:T(8,128)}, u32[]{:S(2)}) copy-start(f32[128,256]{1,0:T(8,128)} %param.12) | copy-start | bytes 393220
  326.7 278.2 %collective-permute-start.3 = (f32[512,3136]{0,1:T(8,128)S(1)}, f32[512,3136]{0,1:T(8,128)S(1)}, u32[]{:S(2)}, u32[]{:S(2)}) collective-permute-start(f32[512,3136]{0,1:T(8,128)S(1)} %add.41), channel_id=1, source_target_pairs={{0,16},{2,18},{4,20},{6,22},{8,24},{10,26},{12,28},{14,30},{16,0},... | collective-permute-start | bytes 19267592 | tf_op jit(solution)/shard_map/ppermute | solution.py:29
  611.3 183.5 %all-reduce.2.cloned.1.call-start = ((), (), s32[]{:S(2)}) async-start(), calls=%async_computation | async-start | bytes 524288 | tf_op jit(solution)/shard_map/psum | solution.py:45
  682.7 21.7 %copy-start.3 = (f32[56,56]{1,0:T(8,128)S(1)}, f32[56,56]{1,0:T(8,128)}, u32[]{:S(2)}) copy-start(f32[56,56]{1,0:T(8,128)} %param.11) | copy-start | bytes 37636
Sparse Core Ops, SparseCore 0:
  611.5 65.0 all-gather.2
  706.0 88.7 all-reduce.1
